TPU v7x, 256 devices: a whole 4x4x8 slice. The times are simulated.
256 devices in a mesh: shard: 8 (over y, core), tensor: 4 (over x), section: 8 (over z).
Axes of the slice: x: 4, y: 4, z: 8, core: 2. Of those that a mesh axis runs over, the one named last changes fastest.
Arguments:
- normed_inputs: bfloat16 [65536, 4096], P(('shard', 'section')), may hold values from -320 to 320
- projection_cotangent: bfloat16 [65536, 2, 1024], P(('shard', 'section'), None, 'tensor'), may hold values from -1 to 1
- small_partials: bfloat16 [64, 10, 4096], P(('shard', 'section'), None, 'tensor'), may hold values from -2000 to 2000
- master_weights: float32 [4096, 2, 1024], P(('shard', 'section'), None, 'tensor'), may hold values from -4 to 4
- first_moment: float32 [4096, 2, 1024], P(('shard', 'section'), None, 'tensor'), may hold values from -3 to 3
- second_moment: float32 [4096, 2, 1024], P(('shard', 'section'), None, 'tensor'), may hold values from 0.05 to 1
- small_master: float32 [10, 4096], P(None, 'tensor'), may hold values from -4 to 4
- small_first: float32 [10, 4096], P(None, 'tensor'), may hold values from -3 to 3
- small_second: float32 [10, 4096], P(None, 'tensor'), may hold values from 0.05 to 1
Outputs:
- updated_master: float32 [4096, 2, 1024], P(('shard', 'section'), None, 'tensor')
- updated_first: float32 [4096, 2, 1024], P(('shard', 'section'), None, 'tensor')
- updated_second: float32 [4096, 2, 1024], P(('shard', 'section'), None, 'tensor')
- gathered_weights: bfloat16 [4096, 2, 1024], P(None, None, 'tensor')
- small_updated_master: float32 [10, 4096], P(None, 'tensor')
- small_updated_first: float32 [10, 4096], P(None, 'tensor')
- small_updated_second: float32 [10, 4096], P(None, 'tensor')
- small_weights: bfloat16 [10, 4096], P(None, 'tensor')
All inputs are finite; a program needn't handle non-finite values.
Results may differ from a plain program's by a relative error of at most 0.0015.
Values may be sent and summed in bfloat16 or wider, within the bound.
A program may use at most 64 MiB of HBM per device.

v0:
```python
import math
import jax
import jax.numpy as jnp
from jax import lax
from jax.sharding import PartitionSpec as P

D = 4096
EXPERTS = 8
STEP = 10
KV_COLS = 1024
SMALL_ROWS = 10
beta_one = 0.9
beta_two = 0.95
learning_rate = 0.01
weight_decay = 0.1
epsilon = 1e-08
clip_factor = 0.5


def adamw(gradient, scale, first, second, master, decay):
    clipped = gradient * scale
    first_new = beta_one * first + (1.0 - beta_one) * clipped
    second_new = beta_two * second + (1.0 - beta_two) * clipped * clipped
    first_hat = first_new / (1.0 - beta_one**STEP)
    second_hat = second_new / (1.0 - beta_two**STEP)
    master_new = master - learning_rate * (
        first_hat / (jnp.sqrt(second_hat) + epsilon) + decay * master
    )
    return (master_new, first_new, second_new)


def body(
    normed_inputs,
    projection_cotangent,
    small_partials,
    master_weights,
    first_moment,
    second_moment,
    small_master,
    small_first,
    small_second,
):
    gradient = lax.psum_scatter(
        jnp.einsum(
            "tf,tjc->fjc", normed_inputs, projection_cotangent, preferred_element_type=jnp.float32
        ),
        ("shard", "section"),
        scatter_dimension=0,
        tiled=True,
    )
    owned_squares = jnp.sum(gradient * gradient)
    local_small = small_partials[0].astype(jnp.float32)
    small_gradient = lax.psum(local_small, ("shard", "section"))
    big_total = lax.psum(owned_squares, ("shard", "tensor", "section"))
    small_total = lax.psum(jnp.sum(small_gradient * small_gradient), "tensor")
    total = big_total + small_total
    limit = clip_factor * math.sqrt(2 * D * KV_COLS + SMALL_ROWS * D)
    scale = jnp.minimum(1.0, limit / (jnp.sqrt(total) + 1e-06))
    master_new, first_new, second_new = adamw(
        gradient, scale, first_moment, second_moment, master_weights, weight_decay
    )
    row_decay = jnp.where(jnp.arange(SMALL_ROWS)[:, None] < EXPERTS, weight_decay, 0.0).astype(
        jnp.float32
    )
    small_master_new, small_first_new, small_second_new = adamw(
        small_gradient, scale, small_first, small_second, small_master, row_decay
    )
    owned_weights = master_new.astype(jnp.bfloat16)
    gathered = lax.all_gather(owned_weights, ("shard", "section"), axis=0, tiled=True)
    return (
        master_new,
        first_new,
        second_new,
        gathered,
        small_master_new,
        small_first_new,
        small_second_new,
        small_master_new.astype(jnp.bfloat16),
    )


def solution(mesh):
    placed = (
        P(("shard", "section"), None),
        P(("shard", "section"), None, "tensor"),
        P(("shard", "section"), None, "tensor"),
        P(("shard", "section"), None, "tensor"),
        P(("shard", "section"), None, "tensor"),
        P(("shard", "section"), None, "tensor"),
        P(None, "tensor"),
        P(None, "tensor"),
        P(None, "tensor"),
    )
    return jax.shard_map(
        body,
        mesh=mesh,
        in_specs=placed,
        out_specs=(
            P(("shard", "section"), None, "tensor"),
            P(("shard", "section"), None, "tensor"),
            P(("shard", "section"), None, "tensor"),
            P(None, None, "tensor"),
            P(None, "tensor"),
            P(None, "tensor"),
            P(None, "tensor"),
            P(None, "tensor"),
        ),
        check_vma=False,
    )
```

profile of v0, /device:TPU:1, one launch (start us, length us, event | category | flops | bytes accessed | tf_op | source)
XLA Modules:
  0.0 454.1 jit_solution(6464595801956574734)
XLA Ops:
  7.2 0.0 copy-start
  7.2 0.0 reduce-scatter.2.cloned.1.call-start
  7.2 1.2 copy-done
  8.4 10.3 %fusion = f32[4096,2,256]{2,0,1:T(8,128)} fusion(bf16[1024,4096]{1,0:T(8,128)(2,1)} %param.9, bf16[1024,2,256]{2,1,0:T(2,128)(2,1)S(1)} %copy-done), kind=kOutput, calls=%fused_computation | convolution fusion | flops 4294967296 | bytes 17825792 | tf_op jit(solution)/shard_map/tf,tjc->fjc/dot_general | solution.py:44
  18.7 0.0 copy-start.1
  18.7 0.0 copy-start.2
  18.8 0.0 copy-start.3
  18.8 0.0 copy-start.4
  18.8 0.0 copy-start.5
  18.8 0.0 copy-start.6
  18.8 0.0 reduce-scatter.2.cloned.1.call-update
  18.8 0.0 all-gather.2.cloned.1.call-start
  18.9 0.6 copy-done.7
  19.5 246.8 %psum.22 = f32[10,1024]{1,0:T(8,128)S(1)} all-reduce(f32[10,1024]{1,0:T(8,128)S(1)} %bitcast_convert_fusion), channel_id=1, replica_groups=mesh['shard'=8,'tensor'=4,'section'=8] {'shard','section'}, use_global_device_ids=true, to_apply=%region_3.0 | all-reduce | flops 10240 | bytes 81920 | tf_op jit(solution)/shard_map/psum | solution.py:53
  266.3 0.6 multiply_reduce_fusion.1
  266.9 1.5 multiply_reduce_fusion
  268.4 9.4 %psum.23 = f32[]{:T(128)} all-reduce(f32[]{:T(128)} %multiply_reduce_fusion.1), channel_id=1, replica_groups=mesh['shard'=8,'tensor'=4,'section'=8] {'tensor'}, use_global_device_ids=true, to_apply=%region_5.0 | all-reduce | flops 1 | bytes 8 | tf_op jit(solution)/shard_map/psum | solution.py:55
  277.9 81.1 %psum.21 = f32[]{:T(128)} all-reduce(f32[]{:T(128)} %multiply_reduce_fusion), channel_id=1, replica_groups=mesh['shard'=8,'tensor'=4,'section'=8] {'shard','tensor','section'}, use_global_device_ids=true, to_apply=%region_2.0 | all-reduce | flops 1 | bytes 8 | tf_op jit(solution)/shard_map/psum | solution.py:54
  360.4 0.0 copy-done.1
  360.4 0.0 copy-done.2
  360.4 0.0 copy-done.3
  360.4 1.7 fusion.8
  362.1 0.0 all-gather.2.cloned.1.call-update
  362.1 0.8 copy.23
  362.9 0.8 copy.24
  363.6 0.8 copy.25
  364.4 0.0 copy-done.4
  364.4 0.0 copy-done.5
  364.4 0.0 copy-done.6
  364.4 0.7 fusion.6
  365.1 72.0 %all-gather.2.cloned.1.call-done = bf16[4096,2,256]{2,0,1:T(8,128)(2,1)} async-done(((bf16[64,2,256]{2,0,1:T(8,128)(2,1)}), bf16[4096,2,256]{2,0,1:T(8,128)(2,1)}) %all-gather.2.cloned.1.call-update) | async-done | bytes 4194320 | tf_op jit(solution)/shard_map/all_gather | solution.py:69
  437.1 10.1 %copy.26 = bf16[4096,2,256]{2,1,0:T(2,128)(2,1)} copy(bf16[4096,2,256]{2,0,1:T(8,128)(2,1)} %all-gather.2.cloned.1.call-done) | data formatting | bytes 8388608
  (4 shorter events, 0.0 us)
Async XLA Ops:
  7.2 1.2 copy-start
  7.2 259.7 %reduce-scatter.2.cloned.1.call-start = ((), (), s32[]{:S(2)}) async-start(), calls=%async_computation.1 | async-start | bytes 8519680 | tf_op jit(solution)/shard_map/reduce_scatter | solution.py:43
  18.7 0.8 copy-start.7
  18.7 341.7 %copy-start.1 = (f32[64,2,256]{2,1,0:T(2,128)S(1)}, f32[64,2,256]{2,1,0:T(2,128)}, u32[]{:S(2)}) copy-start(f32[64,2,256]{2,1,0:T(2,128)} %param.12) | copy-start | bytes 393220
  18.7 341.7 %copy-start.2 = (f32[64,2,256]{2,1,0:T(2,128)S(1)}, f32[64,2,256]{2,1,0:T(2,128)}, u32[]{:S(2)}) copy-start(f32[64,2,256]{2,1,0:T(2,128)} %param.13) | copy-start | bytes 393220
  18.8 341.7 %copy-start.3 = (f32[64,2,256]{2,1,0:T(2,128)S(1)}, f32[64,2,256]{2,1,0:T(2,128)}, u32[]{:S(2)}) copy-start(f32[64,2,256]{2,1,0:T(2,128)} %param.14) | copy-start | bytes 393220
  18.8 345.6 %copy-start.4 = (f32[10,1024]{1,0:T(8,128)S(1)}, f32[10,1024]{1,0:T(8,128)}, u32[]{:S(2)}) copy-start(f32[10,1024]{1,0:T(8,128)} %param.15) | copy-start | bytes 122884
  18.8 345.6 %copy-start.5 = (f32[10,1024]{1,0:T(8,128)S(1)}, f32[10,1024]{1,0:T(8,128)}, u32[]{:S(2)}) copy-start(f32[10,1024]{1,0:T(8,128)} %param.16) | copy-start | bytes 122884
  18.8 345.6 %copy-start.6 = (f32[10,1024]{1,0:T(8,128)S(1)}, f32[10,1024]{1,0:T(8,128)}, u32[]{:S(2)}) copy-start(f32[10,1024]{1,0:T(8,128)} %param.17) | copy-start | bytes 122884
  18.8 418.3 %all-gather.2.cloned.1.call-start = ((), (), s32[]{:S(2)}) async-start(), calls=%async_computation.2 | async-start | bytes 4259840 | tf_op jit(solution)/shard_map/all_gather | solution.py:69
Sparse Core Ops, SparseCore 0:
  18.9 150.9 reduce-scatter.1
  362.2 74.8 all-gather.1
where the time goes:
time: 455 us; the launch traced here: 454 us
  blocking collectives  337 us (74%)
  waiting for transfers between devices  72 us (16%)
  between operations  15.5 us (3%)
  local copies, waits for them, and re-layouts  14.2 us (3%)
  matrix products  10.3 us (2%)
    psum x1, blocking collectives, body(): small_gradient = lax.psum(local_small, ('shard', 'section'))  247 us
    psum x1, blocking collectives, body(): big_total = lax.psum(owned_squares, ('shard', 'tensor', 'section'))  81.1 us
    all_gather x1, waiting for transfers between devices, body(): lax.all_gather(owned_weights, ('shard', 'section'), axis=0, tiled=True)  72 us
    unnamed x20, local copies, waits for them, and re-layouts  14.2 us
    dot_general x1, matrix products, body(): jnp.einsum('tf,tjc->fjc', normed_inputs, projection_cotangent, preferred_...  10.3 us
    psum x1, blocking collectives, body(): small_total = lax.psum(jnp.sum(small_gradient * small_gradient), 'tensor')  9.45 us
  transfers between devices with their start and end apart: 2, of which 1 were waited for; matrix products, arithmetic and copies ran while one was open for 1% of the time, Pallas kernels for 0%

commit v1 on v0

--- a/solution.py
+++ b/solution.py
@@ -50,7 +50,7 @@
     )
     owned_squares = jnp.sum(gradient * gradient)
     local_small = small_partials[0].astype(jnp.float32)
-    small_gradient = lax.psum(local_small, ("shard", "section"))
+    small_gradient = lax.psum(lax.psum(local_small, "section"), "shard")
     big_total = lax.psum(owned_squares, ("shard", "tensor", "section"))
     small_total = lax.psum(jnp.sum(small_gradient * small_gradient), "tensor")
     total = big_total + small_total

time: 455 us -> 357 us (0.78)
  blocking collectives: 337 us -> 145 us
  waiting for transfers between devices: 72 us -> 166 us
    psum x1 -> x2, blocking collectives: 247 us -> 55.6 us  [body(): small_gradient = lax.psum(lax.psum(local_small, 'section'), 'shard')]
    reduce_scatter x1, waiting for transfers between devices: 0.01 us -> 93.6 us  [body(): lax.psum_scatter(jnp.einsum('tf,tjc->fjc', normed_inputs, projection_cota...]
  transfers between devices with their start and end apart: 2 -> 2, of which waited for: 1 -> 2; matrix products, arithmetic and copies ran while one was open for 1% -> 1% of each run, Pallas kernels for 0% -> 0%
where the time goes in v1:
time: 357 us; the launch traced here: 356 us
  waiting for transfers between devices  166 us (46%)
  blocking collectives  145 us (41%)
  between operations  15.5 us (4%)
  local copies, waits for them, and re-layouts  14.2 us (4%)
  matrix products  10.3 us (3%)
  other arithmetic  4.55 us (1%)
    reduce_scatter x1, waiting for transfers between devices, body(): lax.psum_scatter(jnp.einsum('tf,tjc->fjc', normed_inputs, projection_cota...  93.6 us
    psum x1, blocking collectives, body(): big_total = lax.psum(owned_squares, ('shard', 'tensor', 'section'))  81 us
    all_gather x1, waiting for transfers between devices, body(): lax.all_gather(owned_weights, ('shard', 'section'), axis=0, tiled=True)  72.4 us
    psum x2, blocking collectives, body(): small_gradient = lax.psum(lax.psum(local_small, 'section'), 'shard')  55.6 us
    unnamed x20, local copies, waits for them, and re-layouts  14.2 us
    dot_general x1, matrix products, body(): jnp.einsum('tf,tjc->fjc', normed_inputs, projection_cotangent, preferred_...  10.3 us
    psum x1, blocking collectives, body(): small_total = lax.psum(jnp.sum(small_gradient * small_gradient), 'tensor')  8.62 us
  transfers between devices with their start and end apart: 2, of which 2 were waited for; matrix products, arithmetic and copies ran while one was open for 1% of the time, Pallas kernels for 0%

profile of v1, /device:TPU:1, one launch (start us, length us, event | category | flops | bytes accessed | tf_op | source)
XLA Modules:
  0.0 356.0 jit_solution(14598114963233659306)
XLA Ops:
  7.2 0.0 copy-start
  7.2 0.0 reduce-scatter.2.cloned.1.call-start
  7.2 1.2 copy-done
  8.4 10.3 %fusion = f32[4096,2,256]{2,0,1:T(8,128)} fusion(bf16[1024,4096]{1,0:T(8,128)(2,1)} %param.9, bf16[1024,2,256]{2,1,0:T(2,128)(2,1)S(1)} %copy-done), kind=kOutput, calls=%fused_computation | convolution fusion | flops 4294967296 | bytes 17825792 | tf_op jit(solution)/shard_map/tf,tjc->fjc/dot_general | solution.py:44
  18.7 0.0 copy-start.1
  18.8 0.0 copy-start.4
  18.8 0.0 copy-start.5
  18.8 0.0 copy-start.6
  18.8 0.0 reduce-scatter.2.cloned.1.call-update
  18.8 0.0 all-gather.2.cloned.1.call-start
  18.9 0.6 copy-done.7
  19.5 26.9 %psum.29 = f32[10,1024]{1,0:T(8,128)S(1)} all-reduce(f32[10,1024]{1,0:T(8,128)S(1)} %bitcast_convert_fusion), channel_id=1, replica_groups=mesh['shard'=8,'tensor'=4,'section'=8] {'section'}, use_global_device_ids=true, to_apply=%region_3.0 | all-reduce | flops 10240 | bytes 81920 | tf_op jit(solution)/shard_map/psum | solution.py:53
  46.5 28.7 %psum.30 = f32[10,1024]{1,0:T(8,128)S(1)} all-reduce(f32[10,1024]{1,0:T(8,128)S(1)} %psum.29), channel_id=1, replica_groups=mesh['shard'=8,'tensor'=4,'section'=8] {'shard'}, use_global_device_ids=true, to_apply=%region_4.0 | all-reduce | flops 10240 | bytes 81920 | tf_op jit(solution)/shard_map/psum | solution.py:53
  75.1 0.6 multiply_reduce_fusion.1
  75.8 93.6 %reduce-scatter.2.cloned.1.call-done = f32[64,2,256]{2,0,1:T(8,128)} async-done(((f32[4096,2,256]{2,0,1:T(8,128)}), f32[64,2,256]{2,0,1:T(8,128)}) %reduce-scatter.2.cloned.1.call-update) | async-done | bytes 131088 | tf_op jit(solution)/shard_map/reduce_scatter | solution.py:43
  169.4 1.5 multiply_reduce_fusion
  170.9 8.6 %psum.31 = f32[]{:T(128)} all-reduce(f32[]{:T(128)} %multiply_reduce_fusion.1), channel_id=1, replica_groups=mesh['shard'=8,'tensor'=4,'section'=8] {'tensor'}, use_global_device_ids=true, to_apply=%region_6.0 | all-reduce | flops 1 | bytes 8 | tf_op jit(solution)/shard_map/psum | solution.py:55
  179.6 81.0 %psum.28 = f32[]{:T(128)} all-reduce(f32[]{:T(128)} %multiply_reduce_fusion), channel_id=1, replica_groups=mesh['shard'=8,'tensor'=4,'section'=8] {'shard','tensor','section'}, use_global_device_ids=true, to_apply=%region_2.0 | all-reduce | flops 1 | bytes 8 | tf_op jit(solution)/shard_map/psum | solution.py:54
  261.9 0.0 copy-done.1
  261.9 0.0 copy-done.2
  261.9 0.0 copy-done.3
  261.9 1.7 fusion.8
  263.6 0.0 all-gather.2.cloned.1.call-update
  263.6 0.8 copy.23
  264.4 0.8 copy.24
  265.1 0.8 copy.25
  265.9 0.0 copy-done.4
  265.9 0.0 copy-done.5
  265.9 0.0 copy-done.6
  265.9 0.7 fusion.6
  266.6 72.4 %all-gather.2.cloned.1.call-done = bf16[4096,2,256]{2,0,1:T(8,128)(2,1)} async-done(((bf16[64,2,256]{2,0,1:T(8,128)(2,1)}), bf16[4096,2,256]{2,0,1:T(8,128)(2,1)}) %all-gather.2.cloned.1.call-update) | async-done | bytes 4194320 | tf_op jit(solution)/shard_map/all_gather | solution.py:69
  339.0 10.1 %copy.26 = bf16[4096,2,256]{2,1,0:T(2,128)(2,1)} copy(bf16[4096,2,256]{2,0,1:T(8,128)(2,1)} %all-gather.2.cloned.1.call-done) | data formatting | bytes 8388608
  (5 shorter events, 0.0 us)
Async XLA Ops:
  7.2 1.2 copy-start
  7.2 162.2 %reduce-scatter.2.cloned.1.call-start = ((), (), s32[]{:S(2)}) async-start(), calls=%async_computation.1 | async-start | bytes 8519680 | tf_op jit(solution)/shard_map/reduce_scatter | solution.py:43
  18.7 0.8 copy-start.7
  18.7 243.2 %copy-start.1 = (f32[64,2,256]{2,1,0:T(2,128)S(1)}, f32[64,2,256]{2,1,0:T(2,128)}, u32[]{:S(2)}) copy-start(f32[64,2,256]{2,1,0:T(2,128)} %param.12) | copy-start | bytes 393220
  18.7 243.2 %copy-start.2 = (f32[64,2,256]{2,1,0:T(2,128)S(1)}, f32[64,2,256]{2,1,0:T(2,128)}, u32[]{:S(2)}) copy-start(f32[64,2,256]{2,1,0:T(2,128)} %param.13) | copy-start | bytes 393220
  18.8 243.2 %copy-start.3 = (f32[64,2,256]{2,1,0:T(2,128)S(1)}, f32[64,2,256]{2,1,0:T(2,128)}, u32[]{:S(2)}) copy-start(f32[64,2,256]{2,1,0:T(2,128)} %param.14) | copy-start | bytes 393220
  18.8 247.2 %copy-start.4 = (f32[10,1024]{1,0:T(8,128)S(1)}, f32[10,1024]{1,0:T(8,128)}, u32[]{:S(2)}) copy-start(f32[10,1024]{1,0:T(8,128)} %param.15) | copy-start | bytes 122884
  18.8 247.1 %copy-start.5 = (f32[10,1024]{1,0:T(8,128)S(1)}, f32[10,1024]{1,0:T(8,128)}, u32[]{:S(2)}) copy-start(f32[10,1024]{1,0:T(8,128)} %param.16) | copy-start | bytes 122884
  18.8 247.1 %copy-start.6 = (f32[10,1024]{1,0:T(8,128)S(1)}, f32[10,1024]{1,0:T(8,128)}, u32[]{:S(2)}) copy-start(f32[10,1024]{1,0:T(8,128)} %param.17) | copy-start | bytes 122884
  18.8 320.2 %all-gather.2.cloned.1.call-start = ((), (), s32[]{:S(2)}) async-start(), calls=%async_computation.2 | async-start | bytes 4259840 | tf_op jit(solution)/shard_map/all_gather | solution.py:69
Sparse Core Ops, SparseCore 0:
  18.9 150.4 reduce-scatter.1
  263.7 75.2 all-gather.1

commit v2 on v0

--- a/solution.py
+++ b/solution.py
@@ -66,7 +66,15 @@
         small_gradient, scale, small_first, small_second, small_master, row_decay
     )
     owned_weights = master_new.astype(jnp.bfloat16)
-    gathered = lax.all_gather(owned_weights, ("shard", "section"), axis=0, tiled=True)
+    gathered = jnp.concatenate(
+        lax.all_to_all(
+            jnp.stack([owned_weights] * lax.axis_size(("shard", "section"))),
+            ("shard", "section"),
+            0,
+            0,
+        ),
+        axis=0,
+    )
     return (
         master_new,
         first_new,

time: 455 us -> 486 us (1.068)
  waiting for transfers between devices: 72 us -> 93.2 us
  starting transfers between devices: 0.08 us -> 7.01 us
    all_to_all x0 -> x1, waiting for transfers between devices: none -> 93.2 us  [body(): lax.all_to_all(jnp.stack([owned_weights] * lax.axis_size(('shard', 'secti...]
    all_gather x1 -> x0, waiting for transfers between devices: 72 us -> none  [body(): lax.all_gather(owned_weights, ('shard', 'section'), axis=0, tiled=True)]
    all_to_all x0 -> x1, starting transfers between devices: none -> 6.97 us  [body(): lax.all_to_all(jnp.stack([owned_weights] * lax.axis_size(('shard', 'secti...]
    another operation x0 -> x1, local copies, waits for them, and re-layouts: none -> 6.06 us  [body(): jnp.stack([owned_weights] * lax.axis_size(('shard', 'section')))]
where the time goes in v2:
time: 486 us; the launch traced here: 485 us
  blocking collectives  337 us (69%)
  waiting for transfers between devices  93.2 us (19%)
  local copies, waits for them, and re-layouts  18 us (4%)
  between operations  15.5 us (3%)
  matrix products  10.3 us (2%)
  starting transfers between devices  7.01 us (1%)
    psum x1, blocking collectives, body(): small_gradient = lax.psum(local_small, ('shard', 'section'))  247 us
    all_to_all x1, waiting for transfers between devices, body(): lax.all_to_all(jnp.stack([owned_weights] * lax.axis_size(('shard', 'secti...  93.2 us
    psum x1, blocking collectives, body(): big_total = lax.psum(owned_squares, ('shard', 'tensor', 'section'))  81.1 us
    unnamed x20, local copies, waits for them, and re-layouts  11.9 us
    dot_general x1, matrix products, body(): jnp.einsum('tf,tjc->fjc', normed_inputs, projection_cotangent, preferred_...  10.3 us
  transfers between devices with their start and end apart: 2, of which 1 were waited for; matrix products, arithmetic and copies ran while one was open for 1% of the time, Pallas kernels for 0%

profile of v2, /device:TPU:1, one launch (start us, length us, event | category | flops | bytes accessed | tf_op | source)
XLA Modules:
  0.0 485.4 jit_solution(16180263967471010232)
XLA Ops:
  7.2 0.0 copy-start
  7.2 0.0 reduce-scatter.2.cloned.1.call-start
  7.2 1.2 copy-done
  8.4 10.3 %fusion = f32[4096,2,256]{2,0,1:T(8,128)} fusion(bf16[1024,4096]{1,0:T(8,128)(2,1)} %param.9, bf16[1024,2,256]{2,1,0:T(2,128)(2,1)S(1)} %copy-done), kind=kOutput, calls=%fused_computation | convolution fusion | flops 4294967296 | bytes 17825792 | tf_op jit(solution)/shard_map/tf,tjc->fjc/dot_general | solution.py:44
  18.7 0.0 copy-start.7
  18.7 0.0 copy-start.1
  18.7 0.0 copy-start.2
  18.8 0.0 copy-start.3
  18.8 0.0 reduce-scatter.2.cloned.1.call-update
  18.8 0.7 copy-done.7
  19.5 0.0 copy-start.4
  19.5 246.9 %psum.22 = f32[10,1024]{1,0:T(8,128)S(1)} all-reduce(f32[10,1024]{1,0:T(8,128)S(1)} %bitcast_convert_fusion), channel_id=1, replica_groups=mesh['shard'=8,'tensor'=4,'section'=8] {'shard','section'}, use_global_device_ids=true, to_apply=%region_3.0 | all-reduce | flops 10240 | bytes 81920 | tf_op jit(solution)/shard_map/psum | solution.py:53
  266.4 0.6 multiply_reduce_fusion.1
  267.1 1.5 multiply_reduce_fusion
  268.6 9.4 %psum.23 = f32[]{:T(128)} all-reduce(f32[]{:T(128)} %multiply_reduce_fusion.1), channel_id=1, replica_groups=mesh['shard'=8,'tensor'=4,'section'=8] {'tensor'}, use_global_device_ids=true, to_apply=%region_5.0 | all-reduce | flops 1 | bytes 8 | tf_op jit(solution)/shard_map/psum | solution.py:55
  278.0 81.1 %psum.21 = f32[]{:T(128)} all-reduce(f32[]{:T(128)} %multiply_reduce_fusion), channel_id=1, replica_groups=mesh['shard'=8,'tensor'=4,'section'=8] {'shard','tensor','section'}, use_global_device_ids=true, to_apply=%region_2.0 | all-reduce | flops 1 | bytes 8 | tf_op jit(solution)/shard_map/psum | solution.py:54
  360.5 0.0 copy-done.1
  360.5 0.0 copy-done.2
  360.5 0.0 copy-done.3
  360.5 1.0 fusion.8
  361.6 0.1 copy.23
  361.6 6.1 %stack.2 = bf16[64,64,2,256]{3,2,1,0:T(2,128)(2,1)} broadcast(bf16[64,2,256]{2,1,0:T(2,128)(2,1)S(1)} %copy.23), dimensions={1,2,3} | broadcast | bytes 4259840 | tf_op jit(solution)/shard_map/stack | solution.py:71
  367.7 7.0 %all-to-all-start = ((bf16[64,64,2,256]{3,2,1,0:T(2,128)(2,1)}), bf16[64,64,2,256]{3,2,1,0:T(2,128)(2,1)}, u32[]{:S(2)}, u32[]{:S(2)}) async-start(bf16[64,64,2,256]{3,2,1,0:T(2,128)(2,1)} %stack.2), calls=%async_computation.1 | async-start | bytes 8388608 | tf_op jit(solution)/shard_map/all_to_all | solution.py:70
  374.7 0.8 copy.24
  375.5 0.8 copy.25
  376.2 0.8 copy.26
  377.0 0.0 copy-done.4
  377.0 0.0 copy-done.5
  377.0 0.0 copy-done.6
  377.0 0.7 fusion.6
  377.7 93.2 %all-to-all-done = bf16[64,64,2,256]{3,2,1,0:T(2,128)(2,1)} async-done(((bf16[64,64,2,256]{3,2,1,0:T(2,128)(2,1)}), bf16[64,64,2,256]{3,2,1,0:T(2,128)(2,1)}, u32[]{:S(2)}, u32[]{:S(2)}) %all-to-all-start) | async-done | bytes 4194336 | tf_op jit(solution)/shard_map/all_to_all | solution.py:70
  470.9 7.7 %copy.42 = bf16[4096,2,256]{2,1,0:T(2,128)(2,1)} copy(bf16[4096,2,256]{2,1,0:T(2,128)(2,1)} %bitcast.2) | data formatting | bytes 8388608
  (5 shorter events, 0.0 us)
Async XLA Ops:
  7.2 1.2 copy-start
  7.2 259.9 %reduce-scatter.2.cloned.1.call-start = ((), (), s32[]{:S(2)}) async-start(), calls=%async_computation.2 | async-start | bytes 8519680 | tf_op jit(solution)/shard_map/reduce_scatter | solution.py:43
  18.7 0.8 copy-start.7
  18.7 341.8 %copy-start.1 = (f32[64,2,256]{2,1,0:T(2,128)S(1)}, f32[64,2,256]{2,1,0:T(2,128)}, u32[]{:S(2)}) copy-start(f32[64,2,256]{2,1,0:T(2,128)} %param.12) | copy-start | bytes 393220
  18.7 341.8 %copy-start.2 = (f32[64,2,256]{2,1,0:T(2,128)S(1)}, f32[64,2,256]{2,1,0:T(2,128)}, u32[]{:S(2)}) copy-start(f32[64,2,256]{2,1,0:T(2,128)} %param.13) | copy-start | bytes 393220
  18.8 341.8 %copy-start.3 = (f32[64,2,256]{2,1,0:T(2,128)S(1)}, f32[64,2,256]{2,1,0:T(2,128)}, u32[]{:S(2)}) copy-start(f32[64,2,256]{2,1,0:T(2,128)} %param.14) | copy-start | bytes 393220
  19.5 357.5 %copy-start.4 = (f32[10,1024]{1,0:T(8,128)S(1)}, f32[10,1024]{1,0:T(8,128)}, u32[]{:S(2)}) copy-start(f32[10,1024]{1,0:T(8,128)} %param.15) | copy-start | bytes 122884
  19.5 357.5 %copy-start.5 = (f32[10,1024]{1,0:T(8,128)S(1)}, f32[10,1024]{1,0:T(8,128)}, u32[]{:S(2)}) copy-start(f32[10,1024]{1,0:T(8,128)} %param.16) | copy-start | bytes 122884
  19.5 357.5 %copy-start.6 = (f32[10,1024]{1,0:T(8,128)S(1)}, f32[10,1024]{1,0:T(8,128)}, u32[]{:S(2)}) copy-start(f32[10,1024]{1,0:T(8,128)} %param.17) | copy-start | bytes 122884
  367.7 103.2 %all-to-all-start = ((bf16[64,64,2,256]{3,2,1,0:T(2,128)(2,1)}), bf16[64,64,2,256]{3,2,1,0:T(2,128)(2,1)}, u32[]{:S(2)}, u32[]{:S(2)}) async-start(bf16[64,64,2,256]{3,2,1,0:T(2,128)(2,1)} %stack.2), calls=%async_computation.1 | async-start | bytes 8388608 | tf_op jit(solution)/shard_map/all_to_all | solution.py:70
Sparse Core Ops, SparseCore 0:
  18.9 150.7 reduce-scatter.1
